TPU v7x, 32 devices: a whole 2x2x4 slice. The times are simulated.
32 devices in a mesh: row: 4 (over z), col: 8 (over y, x, core).
Axes of the slice: x: 2, y: 2, z: 4, core: 2. Of those that a mesh axis runs over, the one named last changes fastest.
Arguments:
- features: bfloat16 [12288, 128], P(('row', 'col')), may hold values from -6 to 6
- weight: bfloat16 [128, 128], replicated, may hold values from -0.5 to 0.5
- tiles: bfloat16 [4, 2048, 128, 128], P('row', 'col'), may hold values from -0.09375 to 0.09375
- tile_dest: int32 [4, 2048], P('row', 'col'), may hold values from 0 to 23, as said below
- tile_src: int32 [4, 2048], P('row', 'col'), may hold values from 0 to 11, as said below
- tile_count: int32 [4, 8], P('row', 'col'), may hold values from 32 to 256, as said below
- source_of: int32 [12288], P(('row', 'col')), may hold values from 0 to 12287, as said below
- out_grad: bfloat16 [12288, 128], P(('row', 'col')), may hold values from -6 to 6
Outputs:
- activations: bfloat16 [12288, 128], P(('row', 'col'))
- feature_grad: bfloat16 [12288, 128], P(('row', 'col'))
- weight_grad: float32 [128, 128], replicated
Inputs may be any that keep to these rules, and one draw needn't show every extreme that they name: `tile_dest`: the slots of one device name distinct tiles. `tile_src`: the slots of one device name distinct tiles. `tile_count`: some device has all of its 256 slots live. `source_of`: a permutation of the 12288 vertices; of the 384 destination positions of each device, exactly 12 hold source vertices of each device.
All inputs are finite; a program needn't handle non-finite values.
Results may differ from a plain program's by a relative error of at most 0.017.
Values may be sent and summed in bfloat16 or wider, within the bound.
No kernel may reach another device: no remote copies, remote signals or barrier semaphores. Data moves between devices by JAX's collectives and lax.ppermute only.
A program may use at most 64 MiB of HBM per device.

v0:
```python
import math
import jax
import jax.numpy as jnp
from jax import lax
from jax.sharding import PartitionSpec as P


def silu_slope(values):
    sigma = jax.nn.sigmoid(values)
    return sigma * (1.0 + values * (1.0 - sigma))


def tile_products(tile_set, dest_index, source_index, live_count, operand, out_blocks, transposed):
    tile_edge = tile_set.shape[-1]
    feat_width = operand.shape[-1]
    block_size = math.gcd(tile_set.shape[0], 32)
    operand_blocks = operand.reshape(-1, tile_edge, feat_width)
    step_count = (live_count + block_size - 1) // block_size

    def add_block(block_step, totals):
        first_slot = block_step * block_size
        tile_block = lax.dynamic_slice_in_dim(tile_set, first_slot, block_size, 0)
        dest_block = lax.dynamic_slice_in_dim(dest_index, first_slot, block_size, 0)
        source_block = lax.dynamic_slice_in_dim(source_index, first_slot, block_size, 0)
        live_mask = first_slot + jnp.arange(block_size) < live_count
        if transposed:
            product = jnp.einsum(
                "bji,bjf->bif",
                tile_block,
                operand_blocks[dest_block],
                preferred_element_type=jnp.float32,
            )
            target = source_block
        else:
            product = jnp.einsum(
                "bij,bjf->bif",
                tile_block,
                operand_blocks[source_block],
                preferred_element_type=jnp.float32,
            )
            target = dest_block
        product = jnp.where(live_mask[:, None, None], product, 0.0)
        return totals.at[target].add(product)

    totals = jnp.zeros((out_blocks, tile_edge, feat_width), jnp.float32)
    totals = lax.fori_loop(0, step_count, add_block, totals)
    return totals.reshape(-1, feat_width)


def local(features, weight, tiles, tile_dest, tile_src, tile_count, source_of, out_grad):
    shard_rows, feat_width = features.shape
    tile_edge = tiles.shape[-1]
    group_total = lax.axis_size(("row", "col"))
    strip_total = lax.axis_size("row")
    column_total = lax.axis_size("col")
    live_count = tile_count[0, 0]
    hidden = jnp.dot(features, weight, preferred_element_type=jnp.float32).astype(jnp.bfloat16)
    group_rows = lax.all_gather(hidden, "row", axis=0, tiled=True)
    partial_value = tile_products(
        tiles[0],
        tile_dest[0],
        tile_src[0],
        live_count,
        group_rows,
        column_total * shard_rows // tile_edge,
        False,
    )
    own_base = lax.axis_index(("row", "col")) * shard_rows
    summed = lax.psum_scatter(
        partial_value.astype(jnp.bfloat16), "col", scatter_dimension=0, tiled=True
    )
    row_owner = source_of // shard_rows
    send_order = jnp.argsort(row_owner, stable=True)
    got_rows, got_ids = (
        lax.all_to_all(summed[send_order], ("row", "col"), split_axis=0, concat_axis=0, tiled=True),
        lax.all_to_all(
            source_of[send_order], ("row", "col"), split_axis=0, concat_axis=0, tiled=True
        ),
    )
    local_ids = got_ids - own_base
    act_rows = jax.nn.silu(got_rows.astype(jnp.float32)).astype(jnp.bfloat16)
    activations = jnp.zeros((shard_rows, feat_width), jnp.bfloat16).at[local_ids].set(act_rows)
    returned = lax.all_to_all(
        out_grad[local_ids], ("row", "col"), split_axis=0, concat_axis=0, tiled=True
    )
    dest_grad = jnp.zeros((shard_rows, feat_width), jnp.bfloat16).at[send_order].set(returned)
    pre_float = summed.astype(jnp.float32)
    local_grad = (dest_grad.astype(jnp.float32) * silu_slope(pre_float)).astype(jnp.bfloat16)
    strip_grad = lax.all_gather(local_grad, "col", axis=0, tiled=True)
    group_partial = tile_products(
        tiles[0],
        tile_dest[0],
        tile_src[0],
        live_count,
        strip_grad,
        strip_total * shard_rows // tile_edge,
        True,
    )
    source_part = lax.psum_scatter(
        group_partial.astype(jnp.bfloat16), "row", scatter_dimension=0, tiled=True
    )
    feature_grad = jnp.dot(source_part, weight.T, preferred_element_type=jnp.float32).astype(
        jnp.bfloat16
    )
    weight_part = jnp.dot(features.T, source_part, preferred_element_type=jnp.float32)
    weight_grad = lax.psum(weight_part, ("row", "col")) * (
        1.0 / math.sqrt(shard_rows * group_total)
    )
    return (activations, feature_grad, weight_grad)


def solution(mesh):
    placed = (
        P(("row", "col"), None),
        P(),
        P("row", "col", None, None),
        P("row", "col"),
        P("row", "col"),
        P("row", "col"),
        P(("row", "col")),
        P(("row", "col"), None),
    )
    return jax.shard_map(
        local,
        mesh=mesh,
        in_specs=placed,
        out_specs=(P(("row", "col"), None), P(("row", "col"), None), P()),
        check_vma=False,
    )
```

profile of v0, /device:TPU:1, one launch (start us, length us, event | category | flops | bytes accessed | tf_op | source)
XLA Modules:
  0.0 383.0 jit_solution(3259870633152334014)
XLA Ops:
  9.0 14.6 %all_gather.6 = bf16[1536,128]{1,0:T(8,128)(2,1)} all-gather(bf16[384,128]{1,0:T(8,128)(2,1)S(1)} %convolution_convert_fusion.1), channel_id=1, replica_groups=mesh['row'=4,'col'=8] {'row'}, dimensions={0}, use_global_device_ids=true | all-gather | bytes 491520 | tf_op jit(solution)/shard_map/all_gather | solution.py:58
  25.0 10.2 %while.20 = (s32[]{:T(128)}, f32[24,128,128]{2,1,0:T(8,128)}, s32[]{:T(128)}, s32[256]{0:T(256)S(1)}, s32[]{:T(128)}, /*index=5*/bf16[256,128,128]{2,1,0:T(8,128...) while((s32[]{:T(128)}, f32[24,128,128]{2,1,0:T(8,128)}, ...), condition=%wide.region_3.4_spmd, body=%wide.region_1.3_spmd.sunk | while | flops 135267584 | bytes 12588147 | solution.py:46
  25.7 1.7 gather_fusion
  27.5 1.7 convolution_select_fusion.4
  29.1 6.1 %scatter_fusion = f32[24,128,128]{2,1,0:T(8,128)} fusion(f32[24,128,128]{2,1,0:T(8,128)} %get-tuple-element.283, s32[32]{0:T(128)S(1)} %get-tuple-element.258, f32[32,128,128]{2,1,0:T(8,128)S(1)} %convolution_select_fusion.4), kind=kCustom, calls=%fused_computation.5.clone.1 | custom fusion | flops 524288 | bytes 6291584 | tf_op jit(solution)/shard_map/while/body/scatter-add | solution.py:43
  35.2 2.5 convert_element_type.37
  37.8 3.8 sort.17
  41.5 2.8 gather_fusion.2
  45.1 78.3 %all-to-all-start = ((s32[32,12,1]{1,2,0:T(1,128)}), s32[32,12,1]{1,2,0:T(1,128)S(1)}, u32[]{:S(2)}, u32[]{:S(2)}) async-start(s32[32,12,1]{1,2,0:T(1,128)} %bitcast), calls=%async_computation | async-start | bytes 32768 | tf_op jit(solution)/shard_map/all_to_all | solution.py:76
  123.4 6.7 %all-to-all-done = s32[32,12,1]{1,2,0:T(1,128)S(1)} async-done(((s32[32,12,1]{1,2,0:T(1,128)}), s32[32,12,1]{1,2,0:T(1,128)S(1)}, u32[]{:S(2)}, u32[]{:S(2)}) %all-to-all-start) | async-done | bytes 1568 | tf_op jit(solution)/shard_map/all_to_all | solution.py:76
  130.3 1.4 gather_fusion.4
  132.5 2.8 all-to-all-start.2
  135.3 12.0 %copy.18 = bf16[1,256,128,128]{2,3,1,0:T(8,128)(2,1)} copy(bf16[1,256,128,128]{3,2,1,0:T(8,128)(2,1)} %bitcast.28) | data formatting | bytes 16777216 | tf_op args[2]
  147.3 1.5 scatter_custom_fusion.3
  149.8 11.8 %all_gather.7 = bf16[3072,128]{1,0:T(8,128)(2,1)} all-gather(bf16[384,128]{1,0:T(8,128)(2,1)S(1)} %fusion.10), channel_id=1, replica_groups=mesh['row'=4,'col'=8] {'col'}, dimensions={0}, use_global_device_ids=true | all-gather | bytes 884736 | tf_op jit(solution)/shard_map/all_gather | solution.py:89
  161.7 8.3 %while.21 = (s32[]{:T(128)}, f32[12,128,128]{2,1,0:T(8,128)S(1)}, s32[]{:T(128)}, s32[256]{0:T(256)S(1)}, s32[]{:T(128)}, /*index=5*/bf16[256,128,128]{1,2,0:T(8...) while((s32[]{:T(128)}, f32[12,128,128]{2,1,0:T(8,128)S(1)}, ...), condition=%wide.region_9.10_spmd, body=%wide.region_7.9_spmd.sunk | while | flops 135267584 | bytes 12588147 | solution.py:46
  162.5 2.9 gather_fusion.1
  165.4 2.0 convolution_select_fusion.5
  167.4 2.7 scatter_fusion.1
  172.4 71.0 %all_to_all.30 = bf16[32,12,128]{2,1,0:T(8,128)(2,1)S(1)} all-to-all(bf16[32,12,128]{2,1,0:T(8,128)(2,1)S(1)} %all_to_all.22), channel_id=1, replica_groups=mesh['row'=4,'col'=8] {'row','col'}, dimensions={0} | all-to-all | bytes 196608 | tf_op jit(solution)/shard_map/all_to_all | solution.py:75
  243.5 2.1 scatter_custom_fusion.2
  246.5 1.7 convolution_bitcast_fusion
  248.2 1.7 convolution_convert_fusion
  249.9 124.9 %all-reduce.2.cloned.1.call-done = f32[128,128]{0,1:T(8,128)} async-done(((f32[128,128]{0,1:T(8,128)}), f32[128,128]{0,1:T(8,128)}) %all-reduce.2.cloned.1.call-update) | async-done | bytes 65552 | tf_op jit(solution)/shard_map/psum | solution.py:106
  (50 shorter events, 11.5 us)
Async XLA Ops:
  7.2 0.9 copy-start
  7.2 17.8 %copy-start.6 = (s32[1,256]{1,0:T(1,128)S(1)}, s32[1,256]{1,0:T(1,128)}, u32[]{:S(2)}) copy-start(s32[1,256]{1,0:T(1,128)} %param.16) | copy-start | bytes 3076
  7.2 17.8 %copy-start.5 = (s32[1,256]{1,0:T(1,128)S(1)}, s32[1,256]{1,0:T(1,128)}, u32[]{:S(2)}) copy-start(s32[1,256]{1,0:T(1,128)} %param.15) | copy-start | bytes 3076
  7.2 141.6 %reduce-scatter.3.cloned.1.call-start = ((), (), s32[]{:S(2)}) async-start(), calls=%async_computation.5 | async-start | bytes 884736 | tf_op jit(solution)/shard_map/reduce_scatter | solution.py:69
  35.2 2.5 copy-start.1
  37.7 92.6 %copy-start.3 = (bf16[384,128]{1,0:T(8,128)(2,1)S(1)}, bf16[384,128]{1,0:T(8,128)(2,1)}, u32[]{:S(2)}) copy-start(bf16[384,128]{1,0:T(8,128)(2,1)} %param.19) | copy-start | bytes 294916
  45.1 85.1 %all-to-all-start = ((s32[32,12,1]{1,2,0:T(1,128)}), s32[32,12,1]{1,2,0:T(1,128)S(1)}, u32[]{:S(2)}, u32[]{:S(2)}) async-start(s32[32,12,1]{1,2,0:T(1,128)} %bitcast), calls=%async_computation | async-start | bytes 32768 | tf_op jit(solution)/shard_map/all_to_all | solution.py:76
  132.5 14.8 %all-to-all-start.2 = ((bf16[32,12,128]{2,1,0:T(8,128)(2,1)}), bf16[32,12,128]{2,1,0:T(8,128)(2,1)S(1)}, u32[]{:S(2)}, u32[]{:S(2)}) async-start(bf16[32,12,128]{2,1,0:T(8,128)(2,1)} %all_to_all.24), calls=%async_computation.3 | async-start | bytes 262144 | tf_op jit(solution)/shard_map/all_to_all | solution.py:83
  135.3 111.2 %reduce-scatter.5.cloned.1.call-start = ((), (), s32[]{:S(2)}) async-start(), calls=%async_computation.6 | async-start | bytes 491520 | tf_op jit(solution)/shard_map/reduce_scatter | solution.py:99
  170.0 0.9 copy-start.2
  170.0 78.2 %copy-start.4 = (bf16[128,128]{1,0:T(8,128)(2,1)S(1)}, bf16[128,128]{1,0:T(8,128)(2,1)}, u32[]{:S(2)}) copy-start(bf16[128,128]{1,0:T(8,128)(2,1)} %param.13) | copy-start | bytes 98308
  170.9 204.0 %all-reduce.2.cloned.1.call-start = ((), (), s32[]{:S(2)}) async-start(), calls=%async_computation.7 | async-start | bytes 131072 | tf_op jit(solution)/shard_map/psum | solution.py:106
Sparse Core Ops, SparseCore 0:
  37.8 107.7 reduce-scatter.2
  171.0 75.4 reduce-scatter.4
  252.6 122.1 all-reduce.1
where the time goes:
time: 386 us; the launch traced here: 383 us
  waiting for transfers between devices  133 us (34%)
  blocking collectives  97.5 us (25%)
  starting transfers between devices  81.3 us (21%)
  local copies, waits for them, and re-layouts  27.6 us (7%)
  other arithmetic  21.3 us (6%)
  between operations  14.6 us (4%)
  matrix products  7.98 us (2%)
    psum x1, waiting for transfers between devices, local(): lax.psum(weight_part, ('row', 'col'))  125 us
    all_to_all x1, starting transfers between devices, local(): lax.all_to_all(source_of[send_order], ('row', 'col'), split_axis=0, conca...  78.3 us
    all_to_all x1, blocking collectives, local(): lax.all_to_all(summed[send_order], ('row', 'col'), split_axis=0, concat_a...  71 us
    all_gather x1, blocking collectives, local(): group_rows = lax.all_gather(hidden, 'row', axis=0, tiled=True)  14.6 us
    unnamed x16, local copies, waits for them, and re-layouts  12.9 us
    all_gather x1, blocking collectives, local(): strip_grad = lax.all_gather(local_grad, 'col', axis=0, tiled=True)  11.8 us
    scatter-add x2, other arithmetic, add_block(): return totals.at[target].add(product)  8.72 us
  transfers between devices with their start and end apart: 5, of which 3 were waited for; matrix products, arithmetic and copies ran while one was open for 7% of the time, Pallas kernels for 0%

commit v1 on v0

--- a/solution.py
+++ b/solution.py
@@ -103,7 +103,7 @@
         jnp.bfloat16
     )
     weight_part = jnp.dot(features.T, source_part, preferred_element_type=jnp.float32)
-    weight_grad = lax.psum(weight_part, ("row", "col")) * (
+    weight_grad = lax.psum(lax.psum(weight_part, "col"), "row") * (
         1.0 / math.sqrt(shard_rows * group_total)
     )
     return (activations, feature_grad, weight_grad)

time: 386 us -> 352 us (0.912)
  blocking collectives: 97.5 us -> 26.5 us
  starting transfers between devices: 81.3 us -> 142 us
  waiting for transfers between devices: 133 us -> 105 us
    all_to_all x1 -> x0, blocking collectives: 71 us -> none  [local(): lax.all_to_all(summed[send_order], ('row', 'col'), split_axis=0, concat_a...]
    all_to_all x0 -> x1, starting transfers between devices: none -> 60.8 us  [local(): lax.all_to_all(summed[send_order], ('row', 'col'), split_axis=0, concat_a...]
    psum x1 -> x2, waiting for transfers between devices: 125 us -> 86.8 us  [the longest x1 53.9 us: local(): lax.psum(weight_part, 'col')]
    reduce_scatter x1, waiting for transfers between devices: 0.88 us -> 11.6 us  [local(): lax.psum_scatter(group_partial.astype(jnp.bfloat16), 'row', scatter_dimen...]
  transfers between devices with their start and end apart: 5 -> 7, of which waited for: 3 -> 4; matrix products, arithmetic and copies ran while one was open for 7% -> 8% of each run, Pallas kernels for 0% -> 0%
where the time goes in v1:
time: 352 us; the launch traced here: 346 us
  starting transfers between devices  142 us (40%)
  waiting for transfers between devices  105 us (30%)
  local copies, waits for them, and re-layouts  28.3 us (8%)
  blocking collectives  26.5 us (8%)
  other arithmetic  21.3 us (6%)
  between operations  14.6 us (4%)
  matrix products  7.98 us (2%)
    all_to_all x1, starting transfers between devices, local(): lax.all_to_all(source_of[send_order], ('row', 'col'), split_axis=0, conca...  78.3 us
    all_to_all x1, starting transfers between devices, local(): lax.all_to_all(summed[send_order], ('row', 'col'), split_axis=0, concat_a...  60.8 us
    psum x1, waiting for transfers between devices, local(): lax.psum(weight_part, 'col')  53.9 us
    psum x1, waiting for transfers between devices, local(): lax.psum(lax.psum(weight_part, 'col'), 'row')  32.9 us
    all_gather x1, blocking collectives, local(): group_rows = lax.all_gather(hidden, 'row', axis=0, tiled=True)  14.6 us
    unnamed x16, local copies, waits for them, and re-layouts  12.9 us
    all_gather x1, blocking collectives, local(): strip_grad = lax.all_gather(local_grad, 'col', axis=0, tiled=True)  11.8 us
    reduce_scatter x1, waiting for transfers between devices, local(): lax.psum_scatter(group_partial.astype(jnp.bfloat16), 'row', scatter_dimen...  11.6 us
  transfers between devices with their start and end apart: 7, of which 4 were waited for; matrix products, arithmetic and copies ran while one was open for 8% of the time, Pallas kernels for 0%

profile of v1, /device:TPU:1, one launch (start us, length us, event | category | flops | bytes accessed | tf_op | source)
XLA Modules:
  0.0 346.0 jit_solution(11066530294407119655)
XLA Ops:
  9.0 14.6 %all_gather.6 = bf16[1536,128]{1,0:T(8,128)(2,1)} all-gather(bf16[384,128]{1,0:T(8,128)(2,1)S(1)} %convolution_convert_fusion.1), channel_id=1, replica_groups=mesh['row'=4,'col'=8] {'row'}, dimensions={0}, use_global_device_ids=true | all-gather | bytes 491520 | tf_op jit(solution)/shard_map/all_gather | solution.py:58
  25.0 10.2 %while.20 = (s32[]{:T(128)}, f32[24,128,128]{2,1,0:T(8,128)}, s32[]{:T(128)}, s32[256]{0:T(256)S(1)}, s32[]{:T(128)}, /*index=5*/bf16[256,128,128]{2,1,0:T(8,128...) while((s32[]{:T(128)}, f32[24,128,128]{2,1,0:T(8,128)}, ...), condition=%wide.region_3.4_spmd, body=%wide.region_1.3_spmd.sunk | while | flops 135267584 | bytes 12588147 | solution.py:46
  25.7 1.7 gather_fusion
  27.5 1.7 convolution_select_fusion.4
  29.1 6.1 %scatter_fusion = f32[24,128,128]{2,1,0:T(8,128)} fusion(f32[24,128,128]{2,1,0:T(8,128)} %get-tuple-element.283, s32[32]{0:T(128)S(1)} %get-tuple-element.258, f32[32,128,128]{2,1,0:T(8,128)S(1)} %convolution_select_fusion.4), kind=kCustom, calls=%fused_computation.5.clone.1 | custom fusion | flops 524288 | bytes 6291584 | tf_op jit(solution)/shard_map/while/body/scatter-add | solution.py:43
  35.2 2.5 convert_element_type.37
  37.8 3.8 %sort.17 = (s32[384]{0:T(512)}, s32[384]{0:T(512)S(1)}) sort(s32[384]{0:T(512)S(1)} %add_select_fusion, s32[384]{0:T(512)S(1)} %iota.14), dimensions={0}, to_apply=%region_0.1 | sort | flops 3456 | bytes 6144 | tf_op jit(solution)/shard_map/jit(argsort)/sort | solution.py:73
  41.5 2.8 gather_fusion.2
  45.1 78.3 %all-to-all-start = ((s32[32,12,1]{1,2,0:T(1,128)}), s32[32,12,1]{1,2,0:T(1,128)S(1)}, u32[]{:S(2)}, u32[]{:S(2)}) async-start(s32[32,12,1]{1,2,0:T(1,128)} %bitcast), calls=%async_computation | async-start | bytes 32768 | tf_op jit(solution)/shard_map/all_to_all | solution.py:76
  123.4 6.7 %all-to-all-done = s32[32,12,1]{1,2,0:T(1,128)S(1)} async-done(((s32[32,12,1]{1,2,0:T(1,128)}), s32[32,12,1]{1,2,0:T(1,128)S(1)}, u32[]{:S(2)}, u32[]{:S(2)}) %all-to-all-start) | async-done | bytes 1568 | tf_op jit(solution)/shard_map/all_to_all | solution.py:76
  132.5 2.8 all-to-all-start.2
  135.3 12.0 %copy.18 = bf16[1,256,128,128]{2,3,1,0:T(8,128)(2,1)} copy(bf16[1,256,128,128]{3,2,1,0:T(8,128)(2,1)} %bitcast.28) | data formatting | bytes 16777216 | tf_op args[2]
  149.8 11.8 %all_gather.7 = bf16[3072,128]{1,0:T(8,128)(2,1)} all-gather(bf16[384,128]{1,0:T(8,128)(2,1)S(1)} %fusion.10), channel_id=1, replica_groups=mesh['row'=4,'col'=8] {'col'}, dimensions={0}, use_global_device_ids=true | all-gather | bytes 884736 | tf_op jit(solution)/shard_map/all_gather | solution.py:89
  161.7 8.3 %while.21 = (s32[]{:T(128)}, f32[12,128,128]{2,1,0:T(8,128)S(1)}, s32[]{:T(128)}, s32[256]{0:T(256)S(1)}, s32[]{:T(128)}, /*index=5*/bf16[256,128,128]{1,2,0:T(8...) while((s32[]{:T(128)}, f32[12,128,128]{2,1,0:T(8,128)S(1)}, ...), condition=%wide.region_9.10_spmd, body=%wide.region_7.9_spmd.sunk | while | flops 135267584 | bytes 12588147 | solution.py:46
  162.5 2.9 gather_fusion.1
  165.4 2.0 convolution_select_fusion.5
  167.4 2.7 scatter_fusion.1
  173.1 60.8 %all-to-all-start.1 = ((bf16[32,12,128]{2,1,0:T(8,128)(2,1)}), bf16[32,12,128]{2,1,0:T(8,128)(2,1)S(1)}, u32[]{:S(2)}, u32[]{:S(2)}) async-start(bf16[32,12,128]{2,1,0:T(8,128)(2,1)} %all_to_all.22), calls=%async_computation.2 | async-start | bytes 262144 | tf_op jit(solution)/shard_map/all_to_all | solution.py:75
  233.9 11.6 %reduce-scatter.5.cloned.1.call-done = bf16[384,128]{1,0:T(8,128)(2,1)} async-done(((bf16[1536,128]{1,0:T(8,128)(2,1)}), bf16[384,128]{1,0:T(8,128)(2,1)}) %reduce-scatter.5.cloned.1.call-update) | async-done | bytes 98320 | tf_op jit(solution)/shard_map/reduce_scatter | solution.py:99
  245.5 1.7 convolution_bitcast_fusion
  247.3 2.1 scatter_custom_fusion.2
  249.4 53.9 %all-reduce.3.cloned.1.call-done = f32[128,128]{0,1:T(8,128)} async-done(((f32[128,128]{0,1:T(8,128)}), f32[128,128]{0,1:T(8,128)}) %all-reduce.3.cloned.1.call-update) | async-done | bytes 65552 | tf_op jit(solution)/shard_map/psum | solution.py:106
  303.3 1.7 convolution_convert_fusion
  305.0 32.9 %all-reduce.5.cloned.1.call-done = f32[128,128]{0,1:T(8,128)} async-done(((f32[128,128]{0,1:T(8,128)}), f32[128,128]{0,1:T(8,128)}) %all-reduce.5.cloned.1.call-update) | async-done | bytes 65552 | tf_op jit(solution)/shard_map/psum | solution.py:106
  (54 shorter events, 14.3 us)
Async XLA Ops:
  7.2 0.9 copy-start
  7.2 17.8 %copy-start.6 = (s32[1,256]{1,0:T(1,128)S(1)}, s32[1,256]{1,0:T(1,128)}, u32[]{:S(2)}) copy-start(s32[1,256]{1,0:T(1,128)} %param.16) | copy-start | bytes 3076
  7.2 17.8 %copy-start.5 = (s32[1,256]{1,0:T(1,128)S(1)}, s32[1,256]{1,0:T(1,128)}, u32[]{:S(2)}) copy-start(s32[1,256]{1,0:T(1,128)} %param.15) | copy-start | bytes 3076
  7.2 141.6 %reduce-scatter.3.cloned.1.call-start = ((), (), s32[]{:S(2)}) async-start(), calls=%async_computation.5 | async-start | bytes 884736 | tf_op jit(solution)/shard_map/reduce_scatter | solution.py:69
  35.2 2.5 copy-start.1
  37.7 92.6 %copy-start.3 = (bf16[384,128]{1,0:T(8,128)(2,1)S(1)}, bf16[384,128]{1,0:T(8,128)(2,1)}, u32[]{:S(2)}) copy-start(bf16[384,128]{1,0:T(8,128)(2,1)} %param.19) | copy-start | bytes 294916
  45.1 85.1 %all-to-all-start = ((s32[32,12,1]{1,2,0:T(1,128)}), s32[32,12,1]{1,2,0:T(1,128)S(1)}, u32[]{:S(2)}, u32[]{:S(2)}) async-start(s32[32,12,1]{1,2,0:T(1,128)} %bitcast), calls=%async_computation | async-start | bytes 32768 | tf_op jit(solution)/shard_map/all_to_all | solution.py:76
  132.5 14.8 %all-to-all-start.2 = ((bf16[32,12,128]{2,1,0:T(8,128)(2,1)}), bf16[32,12,128]{2,1,0:T(8,128)(2,1)S(1)}, u32[]{:S(2)}, u32[]{:S(2)}) async-start(bf16[32,12,128]{2,1,0:T(8,128)(2,1)} %all_to_all.24), calls=%async_computation.3 | async-start | bytes 262144 | tf_op jit(solution)/shard_map/all_to_all | solution.py:83
  135.3 110.2 %reduce-scatter.5.cloned.1.call-start = ((), (), s32[]{:S(2)}) async-start(), calls=%async_computation.6 | async-start | bytes 491520 | tf_op jit(solution)/shard_map/reduce_scatter | solution.py:99
  170.0 0.9 copy-start.2
  170.0 133.2 %copy-start.4 = (bf16[128,128]{1,0:T(8,128)(2,1)S(1)}, bf16[128,128]{1,0:T(8,128)(2,1)}, u32[]{:S(2)}) copy-start(bf16[128,128]{1,0:T(8,128)(2,1)} %param.13) | copy-start | bytes 98308
  173.1 74.2 %all-to-all-start.1 = ((bf16[32,12,128]{2,1,0:T(8,128)(2,1)}), bf16[32,12,128]{2,1,0:T(8,128)(2,1)S(1)}, u32[]{:S(2)}, u32[]{:S(2)}) async-start(bf16[32,12,128]{2,1,0:T(8,128)(2,1)} %all_to_all.22), calls=%async_computation.2 | async-start | bytes 262144 | tf_op jit(solution)/shard_map/all_to_all | solution.py:75
  233.8 69.4 %all-reduce.3.cloned.1.call-start = ((), (), s32[]{:S(2)}) async-start(), calls=%async_computation.7 | async-start | bytes 131072 | tf_op jit(solution)/shard_map/psum | solution.py:106
  247.2 90.7 %all-reduce.5.cloned.1.call-start = ((), (), s32[]{:S(2)}) async-start(), calls=%async_computation.8 | async-start | bytes 131072 | tf_op jit(solution)/shard_map/psum | solution.py:106
Sparse Core Ops, SparseCore 0:
  37.8 107.7 reduce-scatter.2
  171.0 74.3 reduce-scatter.4
  249.1 54.1 all-reduce.2
  305.4 32.4 all-reduce.4
